TPU v7x, 128 devices: a whole 4x4x4 slice. The times are simulated.
128 devices in a mesh: ctx: 16 (over x, y), head: 8 (over z, core).
Axes of the slice: x: 4, y: 4, z: 4, core: 2. Of those that a mesh axis runs over, the one named last changes fastest.
Arguments:
- query_rows: bfloat16 [32768, 8192], P('ctx', 'head'), may hold values from -0.3984375 to 0.3984375
- key_rows: bfloat16 [32768, 8192], P('ctx', 'head'), may hold values from -6 to 6
- value_rows: bfloat16 [32768, 8192], P('ctx', 'head'), may hold values from -6 to 6
- level_weights: float32 [17, 32, 32768], P(None, 'head', 'ctx'), may hold values from 0.2 to 2
Outputs:
- attended: bfloat16 [32768, 8192], P(('ctx', 'head'))
All inputs are finite; a program needn't handle non-finite values.
Results may differ from a plain program's by a relative error of at most 0.0049.
Values may be sent and summed in bfloat16 or wider, within the bound.
A program may use at most 192 MiB of HBM per device.

v0:
```python
import jax
import jax.numpy as jnp
from jax import lax
from jax.experimental import pallas as pl
from jax.experimental.pallas import tpu as pltpu
from jax.sharding import PartitionSpec as P

MESH = pl.DeviceIdType.MESH
F32 = jnp.float32
BF16 = jnp.bfloat16
BLK = 512
HEADS = 4
DIM = 256
TOKENS = 2048
BLOCKS = TOKENS // BLK
SHARE = 256
TILE = 128
USED_LEVELS = 16
NT = (((1,), (1,)), ((), ()))
TN = (((0,), (0,)), ((), ()))
PEERS = ((2, 0), (2, 1), (1, 0), (1, 1), (3, 0), (3, 1), (0, 1))


def dot(a, b, dims=(((1,), (0,)), ((), ()))):
    return lax.dot_general(a, b, dims, preferred_element_type=F32)


def kernel(
    q_hbm, k_hbm, v_hbm, w_hbm, out_ref,
    q_all, k_all, v_all, w_all, w_rows, w_cols, grid_ref, probs, acc,
    local_states, own, y_send, y_recv, x_send, x_recv, remote, staged,
    in_sem, w_sem, ys_sem, yr_sem, xs_sem, xr_sem, os_sem, or_sem,
):
    ctx = lax.axis_index("ctx")
    me = lax.axis_index("head")
    x, y = ctx // 4, ctx % 4
    z, core = me // 2, me % 2

    barrier = pltpu.get_barrier_semaphore()
    for step in range(1, 4):
        for there in (x * 4 + (y + step) % 4, ((x + step) % 4) * 4 + y):
            pl.semaphore_signal(barrier, inc=1, device_id={"ctx": there}, device_id_type=MESH)
    for dz, dc in PEERS:
        there = ((z + dz) % 4) * 2 + (core + dc) % 2
        pl.semaphore_signal(barrier, inc=1, device_id={"head": there}, device_id_type=MESH)

    def fetch(which, j):
        source = (q_hbm, k_hbm, v_hbm)[which]
        target = (q_all, k_all, v_all)[which]
        columns = pl.ds(pl.multiple_of(j * DIM, DIM), DIM)
        return pltpu.make_async_copy(source.at[:, columns], target.at[j], in_sem.at[which, j])

    fetch(1, 0).start()
    fetch(2, 0).start()
    fetch_w = pltpu.make_async_copy(w_hbm, w_all, w_sem)
    fetch(0, 0).start()
    fetch_w.start()
    for j in range(1, HEADS):
        for which in (1, 2, 0):
            fetch(which, j).start()

    def y_copy(j, step):
        return pltpu.make_async_remote_copy(
            src_ref=y_send.at[j],
            dst_ref=y_recv.at[j, step - 1],
            send_sem=ys_sem.at[j, step - 1],
            recv_sem=yr_sem.at[j, step - 1],
            device_id={"ctx": x * 4 + (y + step) % 4},
            device_id_type=MESH,
        )

    def x_copy(j, step):
        return pltpu.make_async_remote_copy(
            src_ref=x_send.at[j],
            dst_ref=x_recv.at[j, step - 1],
            send_sem=xs_sem.at[j, step - 1],
            recv_sem=xr_sem.at[j, step - 1],
            device_id={"ctx": ((x + step) % 4) * 4 + y},
            device_id_type=MESH,
        )

    def out_copy(j, index):
        dz, dc = PEERS[index]
        there = ((z + dz) % 4) * 2 + (core + dc) % 2
        columns = pl.ds(pl.multiple_of((me * HEADS + j) * DIM, DIM), DIM)
        rows = pl.ds(pl.multiple_of(there * SHARE, SHARE), SHARE)
        return pltpu.make_async_remote_copy(
            src_ref=staged.at[j, rows],
            dst_ref=out_ref.at[:, columns],
            send_sem=os_sem.at[j, index],
            recv_sem=or_sem.at[j, index],
            device_id={"head": there},
            device_id_type=MESH,
        )

    def state_rows(j, index, count):
        return pl.ds(pl.multiple_of((j * 3 + index) * DIM, DIM), count * DIM)

    def make_states(j):
        fetch(1, j).wait()
        fetch(2, j).wait()
        parts = []
        for b in range(BLOCKS):
            rows = pl.ds(b * BLK, BLK)
            parts.append(dot(k_all[j, rows, :], v_all[j, rows, :], TN))
        pair = parts[0] + parts[1]
        for index, state in enumerate((parts[0], pair, parts[2])):
            local_states[state_rows(j, index, 1), :] = state.astype(BF16)
        total = pair + (parts[2] + parts[3])
        own[...] = total
        y_send[j] = total.astype(BF16)

    def send_y(j):
        for step in range(1, 4):
            y_copy(j, step).start()

    def make_weights(j):
        for head in range(HEADS):

            @pl.when(j == head)
            def _():
                for level in range(USED_LEVELS):
                    scale = 2.0 ** (-0.5 * max(level - 1.0, 0.0))
                    w_rows[level : level + 1, :] = w_all[level, head : head + 1, :] * scale

        for part in range(TOKENS // TILE):
            rows = slice(part * TILE, (part + 1) * TILE)
            w_cols[rows, :USED_LEVELS] = w_rows[:, rows].T

    def local_block(j, b):
        base = b * BLK
        half = BLK // 2
        queries = q_all[j, pl.ds(base, BLK), :]
        low = dot(queries, k_all[j, pl.ds(base, half), :], NT)
        high = dot(queries[half:], k_all[j, pl.ds(base + half, half), :], NT)

        def weight(level, start, size):
            return w_cols[base + start : base + start + size, level : level + 1]

        grid = grid_ref[...]
        for tile in range(BLK // TILE):
            start = tile * TILE
            table = jnp.zeros((TILE, TILE), F32)
            for level in range(8):
                table = jnp.where(grid == level, weight(level, start, TILE), table)
            source = low if tile < 2 else high
            first = start % half
            diagonal = source[first : first + TILE, first : first + TILE] * table
            probs[start : start + TILE, start : start + TILE] = diagonal.astype(BF16)
            if tile % 2 == 1:
                beside = source[first : first + TILE, :TILE] * weight(8, start, TILE)
                probs[start : start + TILE, start - TILE : start] = beside.astype(BF16)
        probs[half:, :half] = (low[half:] * weight(9, half, half)).astype(BF16)

        values = v_all[j, pl.ds(base, BLK), :]
        top = dot(probs[:half, :half], values[:half])
        bottom = dot(probs[half:, :], values)

        acc[base : base + half, :] = top
        acc[base + half : base + BLK, :] = bottom
        if b > 0:
            rows = slice(base, base + BLK)
            queries = q_all[j, rows, :].astype(F32)
            bits = [bit for bit in (1, 0) if (b >> bit) & 1]
            left = [(queries * w_cols[rows, 10 + bit : 11 + bit]).astype(BF16) for bit in bits]
            right = local_states[state_rows(j, (0, 0, 1, 1)[b], len(bits)), :]
            acc[rows, :] = acc[rows, :] + dot(jnp.concatenate(left, axis=1), right)

    def exchange_x(j):
        for step in range(1, 4):
            y_copy(j, step).wait_recv()
        total = own[...]
        for step in range(3):
            total = total + y_recv[j, step].astype(F32)
        x_send[j] = total.astype(BF16)
        for step in range(1, 4):

            @pl.when(x + step < 4)
            def _():
                x_copy(j, step).start()

        remote[: 2 * DIM, :] = jnp.zeros((2 * DIM, DIM), BF16)

        @pl.when(y % 2 == 1)
        def _():
            remote[:DIM, :] = y_recv[j, 0]

        @pl.when(y >= 2)
        def _():
            pair = y_recv[j, y - 1].astype(F32) + y_recv[j, y - 2].astype(F32)
            remote[DIM : 2 * DIM, :] = pair.astype(BF16)

    def finish_x(j):
        for step in range(1, 4):

            @pl.when(x >= step)
            def _():
                x_copy(j, step).wait_recv()

        remote[2 * DIM :, :] = jnp.zeros((2 * DIM, DIM), BF16)

        @pl.when(x % 2 == 1)
        def _():
            remote[2 * DIM : 3 * DIM, :] = x_recv[j, 0]

        @pl.when(x >= 2)
        def _():
            pair = x_recv[j, x - 1].astype(F32) + x_recv[j, x - 2].astype(F32)
            remote[3 * DIM :, :] = pair.astype(BF16)

    def finish_share(j, there):
        rows = pl.ds(pl.multiple_of(there * SHARE, SHARE), SHARE)
        queries = q_all[j, rows, :].astype(F32)
        weights = w_cols[rows, :]
        left = jnp.concatenate(
            [(queries * weights[:, 12 + bit : 13 + bit]).astype(BF16) for bit in range(4)], axis=1
        )
        return (acc[rows, :] + dot(left, remote[...])).astype(BF16)

    make_states(0)
    pl.semaphore_wait(barrier, 13)
    send_y(0)

    rows_index = lax.broadcasted_iota(jnp.int32, (TILE, TILE), 0)
    cols_index = lax.broadcasted_iota(jnp.int32, (TILE, TILE), 1)
    xored = jnp.bitwise_xor(rows_index, cols_index)
    grid = jnp.zeros((TILE, TILE), jnp.int32)
    for power in range(7):
        grid = grid + (xored >= 2**power).astype(jnp.int32)
    grid_ref[...] = jnp.where(cols_index <= rows_index, grid, 99)
    probs[...] = jnp.zeros((BLK, BLK), BF16)
    fetch_w.wait()

    @pl.loop(0, HEADS)
    def _(j):
        make_weights(j)
        fetch(0, j).wait()
        local_block(j, 0)
        local_block(j, 1)
        exchange_x(j)

        @pl.when(j + 1 < HEADS)
        def _():
            make_states(j + 1)
            send_y(j + 1)

        local_block(j, 2)
        local_block(j, 3)
        finish_x(j)
        for index, (dz, dc) in enumerate(PEERS):
            there = ((z + dz) % 4) * 2 + (core + dc) % 2
            rows = pl.ds(pl.multiple_of(there * SHARE, SHARE), SHARE)
            staged[j, rows, :] = finish_share(j, there)
            out_copy(j, index).start()
        columns = pl.ds(pl.multiple_of((me * HEADS + j) * DIM, DIM), DIM)
        out_ref[:, columns] = finish_share(j, me)

    @pl.loop(0, HEADS)
    def _(j):
        for step in range(1, 4):
            y_copy(j, step).wait_send()

            @pl.when(x + step < 4)
            def _():
                x_copy(j, step).wait_send()

        for index in range(len(PEERS)):
            out_copy(j, index).wait()


def store(in_ref, out_ref, sem):
    copy = pltpu.make_async_copy(in_ref, out_ref, sem)
    copy.start()
    copy.wait()


def local(query_rows, key_rows, value_rows, level_weights):
    hbm = pl.BlockSpec(memory_space=pl.ANY)
    vmem = pl.BlockSpec(memory_space=pltpu.VMEM)
    dma = pltpu.SemaphoreType.DMA
    width = HEADS * DIM * 8
    gathered = pl.pallas_call(
        kernel,
        out_shape=jax.ShapeDtypeStruct((SHARE, width), BF16),
        in_specs=[hbm] * 4,
        out_specs=vmem,
        scratch_shapes=[
            pltpu.VMEM((HEADS, TOKENS, DIM), BF16),
            pltpu.VMEM((HEADS, TOKENS, DIM), BF16),
            pltpu.VMEM((HEADS, TOKENS, DIM), BF16),
            pltpu.VMEM(level_weights.shape, F32),
            pltpu.VMEM((USED_LEVELS, TOKENS), F32),
            pltpu.VMEM((TOKENS, TILE), F32),
            pltpu.VMEM((TILE, TILE), jnp.int32),
            pltpu.VMEM((BLK, BLK), BF16),
            pltpu.VMEM((TOKENS, DIM), F32),
            pltpu.VMEM((HEADS * 3 * DIM, DIM), BF16),
            pltpu.VMEM((DIM, DIM), F32),
            pltpu.VMEM((HEADS, DIM, DIM), BF16),
            pltpu.VMEM((HEADS, 3, DIM, DIM), BF16),
            pltpu.VMEM((HEADS, DIM, DIM), BF16),
            pltpu.VMEM((HEADS, 3, DIM, DIM), BF16),
            pltpu.VMEM((4 * DIM, DIM), BF16),
            pltpu.VMEM((HEADS, TOKENS, DIM), BF16),
            dma((3, HEADS)),
            dma,
            dma((HEADS, 3)),
            dma((HEADS, 3)),
            dma((HEADS, 3)),
            dma((HEADS, 3)),
            dma((HEADS, len(PEERS))),
            dma((HEADS, len(PEERS))),
        ],
        compiler_params=pltpu.CompilerParams(
            collective_id=0, has_side_effects=True, vmem_limit_bytes=48 * 2**20
        ),
    )(query_rows, key_rows, value_rows, level_weights)
    return pl.pallas_call(
        store,
        out_shape=jax.ShapeDtypeStruct((SHARE, width), BF16),
        in_specs=[vmem],
        out_specs=hbm,
        scratch_shapes=[dma],
    )(gathered)


def solution(mesh):
    in_specs = (P("ctx", "head"), P("ctx", "head"), P("ctx", "head"), P(None, "head", "ctx"))
    out_specs = P(("ctx", "head"), None)
    return jax.shard_map(local, mesh=mesh, in_specs=in_specs, out_specs=out_specs, check_vma=False)
```

profile of v0, /device:TPU:7, one launch (start us, length us, event | category | flops | bytes accessed | tf_op | source)
XLA Modules:
  0.0 76.3 jit_solution(2952881031521352347)
XLA Ops:
  0.0 0.0 copy-start.1
  0.0 1.1 %copy-done.1 = f32[17,4,2048]{2,1,0:T(4,128)S(1)} copy-done((f32[17,4,2048]{2,1,0:T(4,128)S(1)}, f32[17,4,2048]{2,1,0:T(4,128)}, u32[]{:S(2)}) %copy-start.1) | copy-done | bytes 557080
  1.1 69.1 %shard_map.46.in_ref = bf16[256,8192]{1,0:T(8,128)(2,1)S(1)} custom-call(bf16[2048,1024]{1,0:T(8,128)(2,1)} %q_hbm.1, bf16[2048,1024]{1,0:T(8,128)(2,1)} %k_hbm.1, bf16[2048,1024]{1,0:T(8,128)(2,1)} %v_hbm.1, f32[17,4,2048]{2,1,0:T(4,128)S(1)} %copy-done.1), custom_call_target="tpu_custom_call" | custom-call | tf_op jit(solution)/shard_map/pallas_call | solution.py:282
  70.2 0.0 copy-start
  70.2 1.9 %copy-done = bf16[256,8192]{1,0:T(8,128)(2,1)} copy-done((bf16[256,8192]{1,0:T(8,128)(2,1)}, bf16[256,8192]{1,0:T(8,128)(2,1)S(1)}, u32[]{:S(2)}) %copy-start) | copy-done | bytes 4194328
  72.1 4.2 %shard_map.47 = bf16[256,8192]{1,0:T(8,128)(2,1)} custom-call(bf16[256,8192]{1,0:T(8,128)(2,1)} %copy-done), custom_call_target="tpu_custom_call" | custom-call | tf_op jit(solution)/shard_map/pallas_call | solution.py:318
Async XLA Ops:
  0.0 1.1 %copy-start.1 = (f32[17,4,2048]{2,1,0:T(4,128)S(1)}, f32[17,4,2048]{2,1,0:T(4,128)}, u32[]{:S(2)}) copy-start(f32[17,4,2048]{2,1,0:T(4,128)} %w_hbm.1) | copy-start | bytes 1671172
  70.2 1.9 %copy-start = (bf16[256,8192]{1,0:T(8,128)(2,1)}, bf16[256,8192]{1,0:T(8,128)(2,1)S(1)}, u32[]{:S(2)}) copy-start(bf16[256,8192]{1,0:T(8,128)(2,1)S(1)} %shard_map.46.in_ref) | copy-start | bytes 12582916
where the time goes:
time: 76.5 us; the launch traced here: 76.3 us
  Pallas kernels  73.3 us (96%)
  local copies, waits for them, and re-layouts  2.98 us (4%)
    pallas_call x1, Pallas kernels, local(): pl.pallas_call(kernel, out_shape=jax.ShapeDtypeStruct((SHARE, width), BF1...  69.1 us
    pallas_call x1, Pallas kernels, local(): pl.pallas_call(store, out_shape=jax.ShapeDtypeStruct((SHARE, width), BF16...  4.21 us
    unnamed x4, local copies, waits for them, and re-layouts  2.98 us

commit v1 on v0

v1 whole, which is shorter than its diff:
```python
import jax
import jax.numpy as jnp
from jax import lax
from jax.experimental import pallas as pl
from jax.experimental.pallas import tpu as pltpu
from jax.sharding import PartitionSpec as P

MESH = pl.DeviceIdType.MESH
F32 = jnp.float32
BF16 = jnp.bfloat16
BLK = 512
HEADS = 4
DIM = 256
TOKENS = 2048
BLOCKS = TOKENS // BLK
SHARE = 256
TILE = 128
USED_LEVELS = 16
NT = (((1,), (1,)), ((), ()))
TN = (((0,), (0,)), ((), ()))
HALF = DIM // 2
CHUNKS = 2
PIECE = DIM // CHUNKS
PEERS = ((2, 0), (2, 1), (1, 0), (1, 1), (3, 0), (3, 1), (0, 1))


def dot(a, b, dims=(((1,), (0,)), ((), ()))):
    return lax.dot_general(a, b, dims, preferred_element_type=F32)


def kernel(
    q_hbm, k_hbm, v_hbm, w_hbm, out_ref,
    q_all, k_all, v_all, w_all, w_rows, w_cols, grid_ref, probs, acc,
    local_states, y_send, y_recv, x_send, x_recv, remote, staged,
    in_sem, w_sem, ys_sem, yr_sem, xs_sem, xr_sem, os_sem, or_sem,
):
    ctx = lax.axis_index("ctx")
    me = lax.axis_index("head")
    x, y = ctx // 4, ctx % 4
    z, core = me // 2, me % 2

    barrier = pltpu.get_barrier_semaphore()
    for step in range(1, 4):
        for there in (x * 4 + (y + step) % 4, ((x + step) % 4) * 4 + y):
            pl.semaphore_signal(barrier, inc=1, device_id={"ctx": there}, device_id_type=MESH)
    for dz, dc in PEERS:
        there = ((z + dz) % 4) * 2 + (core + dc) % 2
        pl.semaphore_signal(barrier, inc=1, device_id={"head": there}, device_id_type=MESH)

    def fetch(which, j):
        source = (q_hbm, k_hbm, v_hbm)[which]
        target = (q_all, k_all, v_all)[which]
        columns = pl.ds(pl.multiple_of(j * DIM, DIM), DIM)
        return pltpu.make_async_copy(source.at[:, columns], target.at[j], in_sem.at[which, j])

    fetch(1, 0).start()
    fetch(2, 0).start()
    fetch_w = pltpu.make_async_copy(w_hbm, w_all, w_sem)

    def fetch_rest():
        fetch(0, 0).start()
        fetch_w.start()
        for j in range(1, HEADS):
            for which in (1, 2, 0):
                fetch(which, j).start()

    def at(index, start=0, size=DIM):
        return pl.ds(pl.multiple_of(index * DIM + start, PIECE), size)

    def y_copy(j, half, chunk, step):
        index = j * 2 + half
        return pltpu.make_async_remote_copy(
            src_ref=y_send.at[at(index, chunk * PIECE, PIECE)],
            dst_ref=y_recv.at[at(index * 3 + step - 1, chunk * PIECE, PIECE)],
            send_sem=ys_sem.at[index, chunk * 3 + step - 1],
            recv_sem=yr_sem.at[index, chunk * 3 + step - 1],
            device_id={"ctx": x * 4 + (y + step) % 4},
            device_id_type=MESH,
        )

    def x_copy(j, half, chunk, step):
        index = j * 2 + half
        return pltpu.make_async_remote_copy(
            src_ref=x_send.at[at(index, chunk * PIECE, PIECE)],
            dst_ref=x_recv.at[at(index * 3 + step - 1, chunk * PIECE, PIECE)],
            send_sem=xs_sem.at[index, chunk * 3 + step - 1],
            recv_sem=xr_sem.at[index, chunk * 3 + step - 1],
            device_id={"ctx": ((x + step) % 4) * 4 + y},
            device_id_type=MESH,
        )

    def out_columns(j):
        return pl.ds(pl.multiple_of((me * HEADS + j) * DIM, DIM), DIM)

    def out_copy(j, index):
        dz, dc = PEERS[index]
        there = ((z + dz) % 4) * 2 + (core + dc) % 2
        rows = pl.ds(pl.multiple_of(there * SHARE, SHARE), SHARE)
        return pltpu.make_async_remote_copy(
            src_ref=staged.at[j, rows],
            dst_ref=out_ref.at[:, out_columns(j)],
            send_sem=os_sem.at[j, index],
            recv_sem=or_sem.at[j, index],
            device_id={"head": there},
            device_id_type=MESH,
        )

    def make_states(j):
        fetch(1, j).wait()
        fetch(2, j).wait()
        parts = []
        for b in range(BLOCKS):
            rows = pl.ds(b * BLK, BLK)
            parts.append(dot(k_all[j, rows, :], v_all[j, rows, :], TN))
        pair = parts[0] + parts[1]
        zero = jnp.zeros((DIM, DIM), BF16)
        first, second, joint = parts[0].astype(BF16), parts[2].astype(BF16), pair.astype(BF16)
        for b, states in enumerate(((zero, zero), (first, zero), (zero, joint), (second, joint))):
            for bit in range(2):
                start = pl.multiple_of(((j * BLOCKS + b) * 2 + bit) * DIM, DIM)
                local_states[pl.ds(start, DIM), :] = states[bit]
        total = pair + (parts[2] + parts[3])
        for half in range(2):
            y_send[at(j * 2 + half), :] = total[:, half * HALF : (half + 1) * HALF].astype(BF16)

    def send_y(j):
        for half in range(2):
            for chunk in range(CHUNKS):
                for step in range(1, 4):
                    y_copy(j, half, chunk, step).start()

    def make_weights(j):
        for head in range(HEADS):

            @pl.when(j == head)
            def _():
                for level in range(USED_LEVELS):
                    scale = 2.0 ** (-0.5 * max(level - 1.0, 0.0))
                    w_rows[level : level + 1, :] = w_all[level, head : head + 1, :] * scale

        for part in range(TOKENS // TILE):
            rows = slice(part * TILE, (part + 1) * TILE)
            w_cols[rows, :USED_LEVELS] = w_rows[:, rows].T

    def local_block(j, b):
        half = BLK // 2

        def rows(start, size):
            return pl.ds(pl.multiple_of(b * BLK + start, TILE), size)

        queries = q_all[j, rows(0, BLK), :]
        low = dot(queries, k_all[j, rows(0, half), :], NT)
        high = dot(queries[half:], k_all[j, rows(half, half), :], NT)

        def weight(level, start, size):
            return w_cols[rows(start, size), level : level + 1]

        grid = grid_ref[...]
        for tile in range(BLK // TILE):
            start = tile * TILE
            table = jnp.zeros((TILE, TILE), F32)
            for level in range(8):
                table = jnp.where(grid == level, weight(level, start, TILE), table)
            source = low if tile < 2 else high
            first = start % half
            diagonal = source[first : first + TILE, first : first + TILE] * table
            probs[start : start + TILE, start : start + TILE] = diagonal.astype(BF16)
            if tile % 2 == 1:
                beside = source[first : first + TILE, :TILE] * weight(8, start, TILE)
                probs[start : start + TILE, start - TILE : start] = beside.astype(BF16)
        probs[half:, :half] = (low[half:] * weight(9, half, half)).astype(BF16)

        values = v_all[j, rows(0, BLK), :]
        top = dot(probs[:half, :half], values[:half])
        bottom = dot(probs[half:, :], values)
        wide = queries.astype(F32)
        left = [(wide * weight(10 + bit, 0, BLK)).astype(BF16) for bit in range(2)]
        start = pl.multiple_of((j * BLOCKS + b) * 2 * DIM, DIM)
        right = local_states[pl.ds(start, 2 * DIM), :]
        product = dot(jnp.concatenate(left, axis=1), right)
        acc[rows(0, half), :] = top + product[:half]
        acc[rows(half, half), :] = bottom + product[half:]

    def exchange_x(j, half):
        index = j * 2 + half
        for chunk in range(CHUNKS):
            start = chunk * PIECE
            total = y_send[at(index, start, PIECE), :].astype(F32)
            for step in range(1, 4):
                y_copy(j, half, chunk, step).wait_recv()
                arrived = y_recv[at(index * 3 + step - 1, start, PIECE), :]
                total = total + arrived.astype(F32)
            x_send[at(index, start, PIECE), :] = total.astype(BF16)
            for step in range(1, 4):

                @pl.when(x + step < 4)
                def _():
                    x_copy(j, half, chunk, step).start()

        combine(half, 0, y, y_recv, index)

    def combine(half, bit, place, received, index):
        columns = slice(half * HALF, (half + 1) * HALF)
        first = slice(bit * DIM, (bit + 1) * DIM)
        second = slice((bit + 1) * DIM, (bit + 2) * DIM)
        remote[first, columns] = jnp.zeros((DIM, HALF), BF16)
        remote[second, columns] = jnp.zeros((DIM, HALF), BF16)

        @pl.when(place % 2 == 1)
        def _():
            remote[first, columns] = received[at(index * 3), :]

        @pl.when(place >= 2)
        def _():
            pair = received[at(index * 3 + place - 1), :].astype(F32)
            pair = pair + received[at(index * 3 + place - 2), :].astype(F32)
            remote[second, columns] = pair.astype(BF16)

    def finish_x(j, half):
        for chunk in range(CHUNKS):
            for step in range(1, 4):

                @pl.when(x >= step)
                def _():
                    x_copy(j, half, chunk, step).wait_recv()

        combine(half, 2, x, x_recv, j * 2 + half)

    def finish_share(j, there):
        rows = pl.ds(pl.multiple_of(there * SHARE, SHARE), SHARE)
        queries = q_all[j, rows, :].astype(F32)
        weights = w_cols[rows, :]
        left = jnp.concatenate(
            [(queries * weights[:, 12 + bit : 13 + bit]).astype(BF16) for bit in range(4)], axis=1
        )
        return (acc[rows, :] + dot(left, remote[...])).astype(BF16)

    def finish(j, distance):
        for index, (dz, dc) in enumerate(PEERS):
            if dz == distance:
                there = ((z + dz) % 4) * 2 + (core + dc) % 2
                rows = pl.ds(pl.multiple_of(there * SHARE, SHARE), SHARE)
                staged[j, rows, :] = finish_share(j, there)
                out_copy(j, index).start()
        if distance == 0:
            out_ref[:, out_columns(j)] = finish_share(j, me)

    make_states(0)
    fetch_rest()
    pl.semaphore_wait(barrier, 13)
    send_y(0)

    rows_index = lax.broadcasted_iota(jnp.int32, (TILE, TILE), 0)
    cols_index = lax.broadcasted_iota(jnp.int32, (TILE, TILE), 1)
    xored = jnp.bitwise_xor(rows_index, cols_index)
    grid = jnp.zeros((TILE, TILE), jnp.int32)
    for power in range(7):
        grid = grid + (xored >= 2**power).astype(jnp.int32)
    grid_ref[...] = jnp.where(cols_index <= rows_index, grid, 99)
    probs[...] = jnp.zeros((BLK, BLK), BF16)
    fetch_w.wait()

    @pl.loop(0, HEADS)
    def _(j):
        make_weights(j)
        fetch(0, j).wait()
        local_block(j, (z + 2) % 4)
        exchange_x(j, 0)
        exchange_x(j, 1)
        local_block(j, (z + 1) % 4)
        local_block(j, (z + 3) % 4)
        finish_x(j, 0)
        finish_x(j, 1)
        finish(j, 2)
        finish(j, 1)
        finish(j, 3)

        @pl.when(j == 0)
        def _():
            make_states(1)
            send_y(1)

        local_block(j, z)
        finish(j, 0)

        @pl.when(j + 2 < HEADS)
        def _():
            make_states(j + 2)
            send_y(j + 2)

    @pl.loop(0, HEADS)
    def _(j):
        for half in range(2):
            for chunk in range(CHUNKS):
                for step in range(1, 4):
                    y_copy(j, half, chunk, step).wait_send()

                    @pl.when(x + step < 4)
                    def _():
                        x_copy(j, half, chunk, step).wait_send()

        for index in range(len(PEERS)):
            out_copy(j, index).wait()


def store(in_ref, out_ref, sem):
    copy = pltpu.make_async_copy(in_ref, out_ref, sem)
    copy.start()
    copy.wait()


def local(query_rows, key_rows, value_rows, level_weights):
    hbm = pl.BlockSpec(memory_space=pl.ANY)
    vmem = pl.BlockSpec(memory_space=pltpu.VMEM)
    dma = pltpu.SemaphoreType.DMA
    width = HEADS * DIM * 8
    gathered = pl.pallas_call(
        kernel,
        out_shape=jax.ShapeDtypeStruct((SHARE, width), BF16),
        in_specs=[hbm] * 4,
        out_specs=vmem,
        scratch_shapes=[
            pltpu.VMEM((HEADS, TOKENS, DIM), BF16),
            pltpu.VMEM((HEADS, TOKENS, DIM), BF16),
            pltpu.VMEM((HEADS, TOKENS, DIM), BF16),
            pltpu.VMEM(level_weights.shape, F32),
            pltpu.VMEM((USED_LEVELS, TOKENS), F32),
            pltpu.VMEM((TOKENS, TILE), F32),
            pltpu.VMEM((TILE, TILE), jnp.int32),
            pltpu.VMEM((BLK, BLK), BF16),
            pltpu.VMEM((TOKENS, DIM), F32),
            pltpu.VMEM((HEADS * BLOCKS * 2 * DIM, DIM), BF16),
            pltpu.VMEM((HEADS * 2 * DIM, HALF), BF16),
            pltpu.VMEM((HEADS * 6 * DIM, HALF), BF16),
            pltpu.VMEM((HEADS * 2 * DIM, HALF), BF16),
            pltpu.VMEM((HEADS * 6 * DIM, HALF), BF16),
            pltpu.VMEM((4 * DIM, DIM), BF16),
            pltpu.VMEM((HEADS, TOKENS, DIM), BF16),
            dma((3, HEADS)),
            dma,
            dma((HEADS * 2, CHUNKS * 3)),
            dma((HEADS * 2, CHUNKS * 3)),
            dma((HEADS * 2, CHUNKS * 3)),
            dma((HEADS * 2, CHUNKS * 3)),
            dma((HEADS, len(PEERS))),
            dma((HEADS, len(PEERS))),
        ],
        compiler_params=pltpu.CompilerParams(
            collective_id=0, has_side_effects=True, vmem_limit_bytes=96 * 2**19
        ),
    )(query_rows, key_rows, value_rows, level_weights)
    return pl.pallas_call(
        store,
        out_shape=jax.ShapeDtypeStruct((SHARE, width), BF16),
        in_specs=[hbm],
        out_specs=hbm,
        scratch_shapes=[dma],
        compiler_params=pltpu.CompilerParams(vmem_limit_bytes=2**20),
    )(gathered)


def solution(mesh):
    in_specs = (P("ctx", "head"), P("ctx", "head"), P("ctx", "head"), P(None, "head", "ctx"))
    out_specs = P(("ctx", "head"), None)
    return jax.shard_map(local, mesh=mesh, in_specs=in_specs, out_specs=out_specs, check_vma=False)
```

time: 76.5 us -> 70 us (0.915)
  Pallas kernels: 73.3 us -> 68.8 us
  local copies, waits for them, and re-layouts: 2.98 us -> 1.05 us
    pallas_call x1, Pallas kernels: 69.1 us -> 66.8 us  [local(): pl.pallas_call(kernel, out_shape=jax.ShapeDtypeStruct((SHARE, width), BF1...]
    pallas_call x1, Pallas kernels: 4.21 us -> 2.02 us  [local(): pl.pallas_call(store, out_shape=jax.ShapeDtypeStruct((SHARE, width), BF16...]
    unnamed x4 -> x2, local copies, waits for them, and re-layouts: 2.98 us -> 1.05 us
where the time goes in v1:
time: 70 us; the launch traced here: 69.8 us
  Pallas kernels  68.8 us (98%)
  local copies, waits for them, and re-layouts  1.05 us (2%)
    pallas_call x1, Pallas kernels, local(): pl.pallas_call(kernel, out_shape=jax.ShapeDtypeStruct((SHARE, width), BF1...  66.8 us
    pallas_call x1, Pallas kernels, local(): pl.pallas_call(store, out_shape=jax.ShapeDtypeStruct((SHARE, width), BF16...  2.02 us

profile of v1, /device:TPU:7, one launch (start us, length us, event | category | flops | bytes accessed | tf_op | source)
XLA Modules:
  0.0 69.8 jit_solution(10078025838517802672)
XLA Ops:
  0.0 0.0 copy-start
  0.0 1.1 %copy-done = f32[17,4,2048]{2,1,0:T(4,128)S(1)} copy-done((f32[17,4,2048]{2,1,0:T(4,128)S(1)}, f32[17,4,2048]{2,1,0:T(4,128)}, u32[]{:S(2)}) %copy-start) | copy-done | bytes 557080
  1.1 66.8 %shard_map.46.in_ref = bf16[256,8192]{1,0:T(8,128)(2,1)S(1)} custom-call(bf16[2048,1024]{1,0:T(8,128)(2,1)} %q_hbm.1, bf16[2048,1024]{1,0:T(8,128)(2,1)} %k_hbm.1, bf16[2048,1024]{1,0:T(8,128)(2,1)} %v_hbm.1, f32[17,4,2048]{2,1,0:T(4,128)S(1)} %copy-done), custom_call_target="tpu_custom_call" | custom-call | tf_op jit(solution)/shard_map/pallas_call | solution.py:317
  67.8 2.0 %shard_map.47 = bf16[256,8192]{1,0:T(8,128)(2,1)} custom-call(bf16[256,8192]{1,0:T(8,128)(2,1)S(1)} %shard_map.46.in_ref), custom_call_target="tpu_custom_call" | custom-call | tf_op jit(solution)/shard_map/pallas_call | solution.py:352
Async XLA Ops:
  0.0 1.1 %copy-start = (f32[17,4,2048]{2,1,0:T(4,128)S(1)}, f32[17,4,2048]{2,1,0:T(4,128)}, u32[]{:S(2)}) copy-start(f32[17,4,2048]{2,1,0:T(4,128)} %w_hbm.1) | copy-start | bytes 1671172

commit v2 on v1

--- a/solution.py
+++ b/solution.py
@@ -56,10 +56,10 @@
     fetch(1, 0).start()
     fetch(2, 0).start()
     fetch_w = pltpu.make_async_copy(w_hbm, w_all, w_sem)
+    fetch_w.start()
+    fetch(0, 0).start()
 
     def fetch_rest():
-        fetch(0, 0).start()
-        fetch_w.start()
         for j in range(1, HEADS):
             for which in (1, 2, 0):
                 fetch(which, j).start()
@@ -317,7 +317,7 @@
     gathered = pl.pallas_call(
         kernel,
         out_shape=jax.ShapeDtypeStruct((SHARE, width), BF16),
-        in_specs=[hbm] * 4,
+        in_specs=[hbm] * 3 + [pl.BlockSpec(memory_space=pltpu.HBM)],
         out_specs=vmem,
         scratch_shapes=[
             pltpu.VMEM((HEADS, TOKENS, DIM), BF16),
@@ -348,7 +348,7 @@
         compiler_params=pltpu.CompilerParams(
             collective_id=0, has_side_effects=True, vmem_limit_bytes=96 * 2**19
         ),
-    )(query_rows, key_rows, value_rows, level_weights)
+    )(query_rows, key_rows, value_rows, pltpu.with_memory_space_constraint(level_weights, pltpu.HBM))
     return pl.pallas_call(
         store,
         out_shape=jax.ShapeDtypeStruct((SHARE, width), BF16),

time: 70 us -> 69.1 us (0.987)
  local copies, waits for them, and re-layouts: 1.05 us -> 0 us
    unnamed x2 -> x0, local copies, waits for them, and re-layouts: 1.05 us -> none
where the time goes in v2:
time: 69.1 us; the launch traced here: 69 us
  Pallas kernels  69 us (100%)
    pallas_call x1, Pallas kernels, local(): pl.pallas_call(kernel, out_shape=jax.ShapeDtypeStruct((SHARE, width), BF1...  67 us
    pallas_call x1, Pallas kernels, local(): pl.pallas_call(store, out_shape=jax.ShapeDtypeStruct((SHARE, width), BF16...  2.02 us

profile of v2, /device:TPU:7, one launch (start us, length us, event | category | flops | bytes accessed | tf_op | source)
XLA Modules:
  0.0 69.0 jit_solution(238644369343219563)
XLA Ops:
  0.0 67.0 %shard_map.46.in_ref = bf16[256,8192]{1,0:T(8,128)(2,1)S(1)} custom-call(bf16[2048,1024]{1,0:T(8,128)(2,1)} %q_hbm.1, bf16[2048,1024]{1,0:T(8,128)(2,1)} %k_hbm.1, bf16[2048,1024]{1,0:T(8,128)(2,1)} %v_hbm.1, f32[17,4,2048]{2,1,0:T(4,128)} %w_hbm.1), custom_call_target="tpu_custom_call" | custom-call | tf_op jit(solution)/shard_map/pallas_call | solution.py:317
  67.0 2.0 %shard_map.47 = bf16[256,8192]{1,0:T(8,128)(2,1)} custom-call(bf16[256,8192]{1,0:T(8,128)(2,1)S(1)} %shard_map.46.in_ref), custom_call_target="tpu_custom_call" | custom-call | tf_op jit(solution)/shard_map/pallas_call | solution.py:352
